TPU v7x, 256 devices: a whole 4x4x8 slice. The times are simulated.
256 devices in a mesh: ens: 8 (over y, z_hi), tile: 32 (over z_lo, x, core).
Axes of the slice: x: 4, y: 4, z: 8 (z_hi: 2, z_lo: 4; z = z_hi * 4 + z_lo), core: 2. Of those that a mesh axis runs over, the one named last changes fastest.
Arguments:
- fields: bfloat16 [8, 32, 200, 8, 128], P('ens', 'tile'), may hold values from -6 to 6
- target: bfloat16 [8, 32, 200, 8, 128], P('ens', 'tile'), may hold values from -6 to 6
- wet_levels: int32 [32, 8, 128], P('tile'), may hold values from 0 to 19, as said below
- tile_links: int32 [32, 5], replicated, may hold values from -1 to 31, as said below
- tile_owner: int32 [32], replicated, may hold values from 0 to 31, as said below
- kernel: float32 [200, 49], replicated, may hold values from -0.875 to 0.875
- norm_gain: float32 [200], replicated, may hold values from 0.5 to 1.5
- weight_in: bfloat16 [200, 800], replicated, may hold values from -0.4375 to 0.4375
- weight_out: bfloat16 [800, 200], replicated, may hold values from -0.21875 to 0.21875
- layer_scale: float32 [200], replicated, may hold values from 0.25 to 1
Outputs:
- block_out: bfloat16 [8, 32, 200, 8, 128], P('ens', 'tile')
- grad_in: float32 [200, 800], replicated
- grad_out: float32 [800, 200], replicated
- grad_kernel: float32 [200, 49], replicated
Inputs may be any that keep to these rules, and one draw needn't show every extreme that they name: `wet_levels`: 0 is land; a cell is wet at the levels below its value. `tile_links`: the kept tiles are the kept blocks of a grid 8 tiles wide, numbered row by row from the south. West and east wrap around within a grid row; the southmost row has no south neighbour; the northmost row is complete, its north neighbour is the tile of the same row in the mirrored column 7 - column, and only it has flag 1 in column 4; -1 marks a missing neighbour. Column 4 is 0 or 1. `tile_owner`: a permutation.
All inputs are finite; a program needn't handle non-finite values.
Results may differ from a plain program's by a relative error of at most 0.005.
Values may be sent and summed in bfloat16 or wider, within the bound.
No kernel may reach another device: no remote copies, remote signals or barrier semaphores. Data moves between devices by JAX's collectives and lax.ppermute only.
A program may use at most 192 MiB of HBM per device.

v0:
```python
import jax
import jax.numpy as jnp
from jax import lax
from jax.sharding import PartitionSpec as P

LEVELS = 19
root_half = 0.7071067811865476
gauss_norm = 0.3989422804014327
norm_epsilon = 1e-06


def gelu_value(values):
    return 0.5 * values * (1.0 + lax.erf(values * root_half))


def gelu_slope(values):
    return (
        0.5 * (1.0 + lax.erf(values * root_half))
        + values * jnp.exp(-0.5 * values * values) * gauss_norm
    )


def take_slot(held, pieces, slot_id):
    piece_count = pieces.shape[0]
    inside = (slot_id >= 0) & (slot_id >= 0) & (slot_id < piece_count)
    taken = lax.dynamic_index_in_dim(
        pieces, jnp.clip(slot_id, 0, piece_count - 1), 0, keepdims=False
    )
    return jnp.where(inside, taken, held)


def local(
    fields,
    target,
    wet_levels,
    tile_links,
    tile_owner,
    kernel,
    norm_gain,
    weight_in,
    weight_out,
    layer_scale,
):
    members, _, channels, row_count, col_count = fields.shape
    tile_count = tile_owner.shape[0]
    own_slot = lax.axis_index("tile")
    own_tile = jnp.sum(
        jnp.where(tile_owner == own_slot, jnp.arange(tile_count, dtype=jnp.int32), 0)
    )
    level_of = jnp.arange(channels, dtype=jnp.int32) * LEVELS // channels
    wet_mask = wet_levels[0][None, :, :] > level_of[:, None, None]
    own_input = fields[:, 0]
    masked = jnp.where(wet_mask[None], own_input, jnp.zeros_like(own_input))
    entry_total = jnp.float32(
        members * lax.axis_size("ens") * tile_count * channels * row_count * col_count
    )

    def link_of(tile_id, column):
        return jnp.where(tile_id >= 0, tile_links[jnp.clip(tile_id, 0, tile_count - 1), column], -1)

    def slot_of(tile_id):
        return jnp.where(tile_id >= 0, tile_owner[jnp.clip(tile_id, 0, tile_count - 1)], -1)

    north_slot = slot_of(link_of(own_tile, 0))
    south_slot = slot_of(link_of(own_tile, 1))
    own_fold = link_of(own_tile, 4)
    west_tile = link_of(own_tile, 2)
    east_tile = link_of(own_tile, 3)
    west_slot = slot_of(west_tile)
    east_slot = slot_of(east_tile)
    zero_rows = jnp.zeros((members, channels, 3, col_count), jnp.bfloat16)
    row_strips = jnp.stack([masked[:, :, :3, :], masked[:, :, row_count - 3 :, :]], axis=0)[None]
    held = (zero_rows, zero_rows, zero_rows)
    pieces = lax.all_gather(row_strips, "tile", axis=0, tiled=True)
    lower_rows = take_slot(held[0], pieces[:, 0], north_slot)
    upper_rows = take_slot(held[1], pieces[:, 1], north_slot)
    below_rows = take_slot(held[2], pieces[:, 1], south_slot)
    north_rows = jnp.where(own_fold == 1, jnp.flip(upper_rows, (2, 3)), lower_rows)
    center = jnp.concatenate([below_rows, masked, north_rows], axis=2)
    side_cols = jnp.swapaxes(
        jnp.stack([center[..., :3], center[..., col_count - 3 :]], axis=0), 3, 4
    )[None]
    zero_cols = jnp.zeros((members, channels, 3, row_count + 6), jnp.bfloat16)
    held = (zero_cols, zero_cols)
    pieces = lax.all_gather(side_cols, "tile", axis=0, tiled=True)
    west_part = take_slot(held[0], pieces[:, 1], west_slot)
    east_part = take_slot(held[1], pieces[:, 0], east_slot)
    west_cols = jnp.swapaxes(west_part, 2, 3)
    east_cols = jnp.swapaxes(east_part, 2, 3)
    extended = jnp.concatenate([west_cols, center, east_cols], axis=3).astype(jnp.float32)
    conv_out = jnp.zeros((members, channels, row_count, col_count), jnp.float32)
    for row_off in range(7):
        for col_off in range(7):
            conv_out = (
                conv_out
                + kernel[:, 7 * row_off + col_off][None, :, None, None]
                * extended[:, :, row_off : row_off + row_count, col_off : col_off + col_count]
            )
    chan_mean = jnp.mean(conv_out, axis=1, keepdims=True)
    chan_var = jnp.mean((conv_out - chan_mean) ** 2, axis=1, keepdims=True)
    inv_std = 1.0 / jnp.sqrt(chan_var + norm_epsilon)
    centred = (conv_out - chan_mean) * inv_std
    gain_wide = norm_gain[None, :, None, None]
    scale_wide = layer_scale[None, :, None, None]
    normed = (centred * gain_wide).astype(jnp.bfloat16)
    flat_norm = normed.reshape(members, channels, row_count * col_count)
    hidden = jnp.einsum("ch,ecp->ehp", weight_in, flat_norm, preferred_element_type=jnp.float32)
    activated = gelu_value(hidden).astype(jnp.bfloat16)
    mlp_out = jnp.einsum("hc,ehp->ecp", weight_out, activated, preferred_element_type=jnp.float32)
    mlp_out = mlp_out.reshape(members, channels, row_count, col_count)
    block_out = (masked.astype(jnp.float32) + scale_wide * mlp_out).astype(jnp.bfloat16)
    misfit = jnp.where(
        wet_mask[None], block_out.astype(jnp.float32) - target[:, 0].astype(jnp.float32), 0.0
    )
    grad_mlp = (
        (2.0 * scale_wide * misfit)
        .astype(jnp.bfloat16)
        .reshape(members, channels, row_count * col_count)
    )
    part_out = jnp.einsum("ehp,ecp->hc", activated, grad_mlp, preferred_element_type=jnp.float32)
    grad_act = jnp.einsum("hc,ecp->ehp", weight_out, grad_mlp, preferred_element_type=jnp.float32)
    grad_hidden = (grad_act * gelu_slope(hidden)).astype(jnp.bfloat16)
    part_in = jnp.einsum("ecp,ehp->ch", flat_norm, grad_hidden, preferred_element_type=jnp.float32)
    grad_normed = jnp.einsum(
        "ch,ehp->ecp", weight_in, grad_hidden, preferred_element_type=jnp.float32
    )
    grad_scaled = grad_normed.reshape(members, channels, row_count, col_count) * gain_wide
    grad_conv = (
        grad_scaled
        - jnp.mean(grad_scaled, axis=1, keepdims=True)
        - centred * jnp.mean(grad_scaled * centred, axis=1, keepdims=True)
    ) * inv_std
    kernel_terms = []
    for row_off in range(7):
        for col_off in range(7):
            kernel_terms.append(
                jnp.sum(
                    grad_conv
                    * extended[:, :, row_off : row_off + row_count, col_off : col_off + col_count],
                    axis=(0, 2, 3),
                )
            )
    part_kernel = jnp.stack(kernel_terms, axis=1)
    sum_in, sum_out, sum_kernel = lax.psum((part_in, part_out, part_kernel), ("ens", "tile"))
    return (
        block_out[:, None],
        sum_in / entry_total,
        sum_out / entry_total,
        sum_kernel / entry_total,
    )


def solution(mesh):
    placed = (
        P("ens", "tile", None, None, None),
        P("ens", "tile", None, None, None),
        P("tile", None, None),
        P(),
        P(),
        P(),
        P(),
        P(),
        P(),
        P(),
    )
    return jax.shard_map(
        local,
        mesh=mesh,
        in_specs=placed,
        out_specs=(P("ens", "tile", None, None, None), P(), P(), P()),
        check_vma=False,
    )
```

profile of v0, /device:TPU:8, one launch (start us, length us, event | category | flops | bytes accessed | tf_op | source)
XLA Modules:
  0.0 526.0 jit_solution(14262006590394135632)
XLA Ops:
  7.2 1.2 compare_select_fusion.2
  9.4 1.3 fusion.30
  12.0 1.5 constant_dynamic-slice_fusion.3
  16.0 1.5 fusion.43
  19.4 65.3 %all-gather.5.cloned.1.call-done = bf16[64,1,200,3,128]{4,2,3,1,0:T(8,128)(2,1)} async-done(((bf16[2,1,200,3,128]{4,2,3,1,0:T(8,128)(2,1)}), bf16[64,1,200,3,128]{4,2,3,1,0:T(8,128)(2,1)}) %all-gather.5.cloned.1.call-update) | async-done | bytes 9830416 | tf_op jit(solution)/shard_map/all_gather | solution.py:74
  84.7 9.3 %fusion.39 = (bf16[32,1,1,200,3,128]{5,3,4,2,1,0:T(8,128)(2,1)}, bf16[32,1,1,200,3,128]{5,3,4,2,1,0:T(8,128)(2,1)}) fusion(bf16[32,2,1,200,3,128]{5,3,4,2,1,0:T(8,128)(2,1)} %bitcast.230), kind=kLoop, calls=%fused_computation.131 | loop fusion | bytes 19660800 | tf_op jit(solution)/shard_map/slice | solution.py:75
  94.1 1.0 select_bitcast_fusion.3
  95.1 0.9 rev.4
  96.1 1.0 bitcast_select_fusion
  97.8 1.3 copy.28
  100.7 0.9 squeeze.55
  101.6 1.1 reshape.540
  105.3 52.3 %all-gather.7.cloned.1.call-done = bf16[64,1,200,3,14]{2,4,3,1,0:T(8,128)(2,1)} async-done(((bf16[2,1,200,3,14]{2,4,3,1,0:T(8,128)(2,1)}), bf16[64,1,200,3,14]{2,4,3,1,0:T(8,128)(2,1)}) %all-gather.7.cloned.1.call-update) | async-done | bytes 1075216 | tf_op jit(solution)/shard_map/all_gather | solution.py:85
  157.6 28.8 %copy.29 = bf16[64,1,200,3,14]{3,2,4,0,1:T(8,128)(2,1)} copy(bf16[64,1,200,3,14]{2,4,3,1,0:T(8,128)(2,1)} %all-gather.7.cloned.1.call-done) | data formatting | bytes 2150400 | tf_op jit(solution)/shard_map/all_gather | solution.py:85
  186.4 30.0 %fusion.38 = (bf16[32,1,1,200,3,14]{4,3,5,2,1,0:T(8,128)(2,1)}, bf16[32,1,1,200,3,14]{4,3,5,2,1,0:T(8,128)(2,1)}) fusion(bf16[32,2,1,200,3,14]{4,3,5,2,1,0:T(8,128)(2,1)} %bitcast.229), kind=kLoop, calls=%fused_computation.130 | loop fusion | bytes 2150400 | tf_op jit(solution)/shard_map/slice | solution.py:86
  216.3 1.4 select_bitcast_fusion
  218.1 1.8 maximum_convert_fusion
  220.3 11.7 %fusion.37 = (f32[8,128]{1,0:T(8,128)S(1)}, f32[1,200,8,128]{3,1,2,0:T(8,128)S(1)}) fusion(f32[1,200,14,134]{3,1,2,0:T(8,128)S(1)} %maximum_convert_fusion, f32[200]{0:T(256)S(1)} %bitcast.247, f32[200]{0:T(256)S(1)} %bitcast.248, f32[200]{0:T(256)S(1)} %bitcast.250, f32[200]{0:T(256)S(1)} %bitcast.251, f32[200]{0:T(256)S(1)} %bitcast.252, ...), kind=kLoop, calls=%fused_computation.129 | loop fusion | flops 20069376 | bytes 41003296 | tf_op jit(solution)/shard_map/reduce_sum | solution.py:99
  233.4 1.5 fusion.28
  236.1 1.7 fusion.5
  237.8 1.8 fusion.26
  239.6 1.5 fusion.17
  241.1 1.6 fusion.13
  242.7 1.6 multiply_reduce_fusion.49
  244.3 6.1 %multiply_reduce_fusion = (f32[200]{0:T(256)S(1)}, f32[200]{0:T(256)S(1)}, f32[200]{0:T(256)S(1)}, f32[200]{0:T(256)S(1)}, f32[200]{0:T(256)S(1)}, /*index=5*/f3...) fusion(f32[1,200,14,134]{3,1,2,0:T(8,128)S(1)} %maximum_convert, ...), kind=kLoop, calls=%fused_computation.30 | loop fusion | flops 8802800 | bytes 17234784 | tf_op jit(solution)/shard_map/reduce_sum | solution.py:137
  251.3 4.7 multiply_reduce_fusion.18
  256.1 4.6 multiply_reduce_fusion.36
  261.0 76.9 %psum.23 = f32[200,49]{0,1:T(8,128)S(1)} all-reduce(f32[200,49]{0,1:T(8,128)S(1)} %stack.223), channel_id=1, replica_groups=mesh['ens'=8,'tile'=32] {'ens','tile'}, use_global_device_ids=true, to_apply=%region_56.57 | all-reduce | flops 9800 | bytes 78400 | tf_op jit(solution)/shard_map/psum | solution.py:144
  338.5 2.4 add_convert_fusion
  340.9 174.4 %all-reduce.3.cloned.1.call-done = (f32[200,800]{1,0:T(8,128)}, f32[800,200]{0,1:T(8,128)}) async-done(((f32[200,800]{1,0:T(8,128)}, f32[800,200]{0,1:T(8,128)}), (f32[200,800]{1,0:T(8,128)}, f32[800,200]{0,1:T(8,128)})) %all-reduce.3.cloned.1.call-update) | async-done | bytes 1280016 | tf_op jit(solution)/shard_map/psum | solution.py:144
  515.4 2.0 broadcast_multiply_fusion
  517.4 2.0 broadcast_multiply_fusion.1
  (136 shorter events, 8.9 us)
Async XLA Ops:
  7.2 225.3 %copy-start = (bf16[200,800]{1,0:T(8,128)(2,1)S(1)}, bf16[200,800]{1,0:T(8,128)(2,1)}, u32[]{:S(2)}) copy-start(bf16[200,800]{1,0:T(8,128)(2,1)} %param.17) | copy-start | bytes 960004
  7.2 77.5 %all-gather.5.cloned.1.call-start = ((), (), s32[]{:S(2)}) async-start(), calls=%async_computation | async-start | bytes 10137600 | tf_op jit(solution)/shard_map/all_gather | solution.py:74
  8.5 88.6 %copy-start.3 = (bf16[1,200,8,128]{3,1,2,0:T(8,128)(2,1)}, bf16[1,200,8,128]{3,1,2,0:T(8,128)(2,1)S(1)}, u32[]{:S(2)}) copy-start(bf16[1,200,8,128]{3,1,2,0:T(8,128)(2,1)S(1)} %compare_select_fusion.2) | copy-start | bytes 1228804
  9.3 148.2 %all-gather.7.cloned.1.call-start = ((), (), s32[]{:S(2)}) async-start(), calls=%async_computation.1 | async-start | bytes 1622016 | tf_op jit(solution)/shard_map/all_gather | solution.py:85
  97.1 3.5 copy-start.4
  97.4 4.2 copy-start.9
  97.4 5.3 %copy-start.12 = (f32[200]{0:T(256)S(1)}, f32[200]{0:T(256)}, u32[]{:S(2)}) copy-start(f32[200]{0:T(256)} %param.19) | copy-start | bytes 2404
  97.5 5.8 %copy-start.10 = (f32[200,49]{0,1:T(8,128)S(1)}, f32[200,49]{0,1:T(8,128)}, u32[]{:S(2)}) copy-start(f32[200,49]{0,1:T(8,128)} %param.15) | copy-start | bytes 117604
  99.2 416.2 %all-reduce.3.cloned.1.call-start = ((), (), s32[]{:S(2)}) async-start(), calls=%async_computation.2 | async-start | bytes 2867200 | tf_op jit(solution)/shard_map/psum | solution.py:144
  217.8 2.2 copy-start.14
  217.8 2.2 copy-start.15
  217.8 2.2 copy-start.16
  217.8 2.2 copy-start.17
  217.8 2.2 copy-start.18
  217.8 2.2 copy-start.19
  217.8 2.2 copy-start.20
  217.8 2.2 copy-start.21
  217.8 2.2 copy-start.22
  217.9 2.2 copy-start.23
  217.9 2.2 copy-start.24
  217.9 2.2 copy-start.25
  217.9 2.2 copy-start.26
  217.9 2.2 copy-start.27
  217.9 2.2 copy-start.28
  217.9 2.2 copy-start.29
  217.9 2.2 copy-start.30
  220.3 11.9 %copy-start.13 = (f32[200]{0:T(256)S(1)}, f32[200]{0:T(256)}, u32[]{:S(2)}) copy-start(f32[200]{0:T(256)} %param.16) | copy-start | bytes 2404
  233.3 2.4 copy-start.5
  233.4 2.4 copy-start.8
  233.4 2.4 copy-start.11
  233.4 2.4 copy-start.52
  256.1 4.6 copy-start.7
  (25 other events, 50.0 us)
Sparse Core Ops, SparseCore 0:
  10.4 74.2 all-gather.4
  99.3 58.2 all-gather.6
  256.2 259.1 all-reduce.2
where the time goes:
time: 528 us; the launch traced here: 526 us
  waiting for transfers between devices  292 us (55%)
  local copies, waits for them, and re-layouts  80.3 us (15%)
  blocking collectives  76.9 us (15%)
  other arithmetic  45.9 us (9%)
  between operations  21.6 us (4%)
  matrix products  8.73 us (2%)
    psum x1, waiting for transfers between devices, local(): lax.psum((part_in, part_out, part_kernel), ('ens', 'tile'))  174 us
    psum x1, blocking collectives, local(): lax.psum((part_in, part_out, part_kernel), ('ens', 'tile'))  76.9 us
    all_gather x1, waiting for transfers between devices, local(): pieces = lax.all_gather(row_strips, 'tile', axis=0, tiled=True)  65.3 us
    all_gather x1, waiting for transfers between devices, local(): pieces = lax.all_gather(side_cols, 'tile', axis=0, tiled=True)  52.3 us
    slice x1, local copies, waits for them, and re-layouts, local(): west_part = take_slot(held[0], pieces[:, 1], west_slot)  30 us
    all_gather x1, local copies, waits for them, and re-layouts, local(): pieces = lax.all_gather(side_cols, 'tile', axis=0, tiled=True)  28.8 us
    reduce_sum x3, other arithmetic, local(): jnp.sum(grad_conv * extended[:, :, row_off:row_off + row_count, col_off:c...  15.4 us
    reduce_sum x1, other arithmetic, local(): chan_mean = jnp.mean(conv_out, axis=1, keepdims=True)  11.7 us
  transfers between devices with their start and end apart: 3, of which 3 were waited for; matrix products, arithmetic and copies ran while one was open for 3% of the time, Pallas kernels for 0%

commit v1 on v0

--- a/solution.py
+++ b/solution.py
@@ -7,6 +7,12 @@
 root_half = 0.7071067811865476
 gauss_norm = 0.3989422804014327
 norm_epsilon = 1e-06
+
+
+def write_sheets_on(panel):
+    for at in ("ens", "tile"):
+        panel = lax.psum(panel, at)
+    return panel
 
 
 def gelu_value(values):
@@ -141,7 +147,7 @@
                 )
             )
     part_kernel = jnp.stack(kernel_terms, axis=1)
-    sum_in, sum_out, sum_kernel = lax.psum((part_in, part_out, part_kernel), ("ens", "tile"))
+    sum_in, sum_out, sum_kernel = write_sheets_on((part_in, part_out, part_kernel))
     return (
         block_out[:, None],
         sum_in / entry_total,

time: 528 us -> 682 us (1.29)
  blocking collectives: 76.9 us -> 184 us
  waiting for transfers between devices: 292 us -> 339 us
    psum x1 -> x2, blocking collectives: 76.9 us -> 184 us  [write_sheets_on(): panel = lax.psum(panel, at)]
    psum x1 -> x2, waiting for transfers between devices: 174 us -> 221 us  [write_sheets_on(): panel = lax.psum(panel, at)]
  transfers between devices with their start and end apart: 3 -> 4, of which waited for: 3 -> 4; matrix products, arithmetic and copies ran while one was open for 3% -> 4% of each run, Pallas kernels for 0% -> 0%
where the time goes in v1:
time: 682 us; the launch traced here: 679 us
  waiting for transfers between devices  339 us (50%)
  blocking collectives  184 us (27%)
  local copies, waits for them, and re-layouts  81.5 us (12%)
  other arithmetic  43.7 us (6%)
  between operations  21.7 us (3%)
  matrix products  9.32 us (1%)
    psum x2, waiting for transfers between devices, write_sheets_on(): panel = lax.psum(panel, at)  221 us
    psum x2, blocking collectives, write_sheets_on(): panel = lax.psum(panel, at)  184 us
    all_gather x1, waiting for transfers between devices, local(): pieces = lax.all_gather(row_strips, 'tile', axis=0, tiled=True)  65.3 us
    all_gather x1, waiting for transfers between devices, local(): pieces = lax.all_gather(side_cols, 'tile', axis=0, tiled=True)  52.3 us
    slice x1, local copies, waits for them, and re-layouts, local(): west_part = take_slot(held[0], pieces[:, 1], west_slot)  30 us
    all_gather x1, local copies, waits for them, and re-layouts, local(): pieces = lax.all_gather(side_cols, 'tile', axis=0, tiled=True)  28.8 us
    reduce_sum x3, other arithmetic, local(): jnp.sum(grad_conv * extended[:, :, row_off:row_off + row_count, col_off:c...  14.5 us
  transfers between devices with their start and end apart: 4, of which 4 were waited for; matrix products, arithmetic and copies ran while one was open for 4% of the time, Pallas kernels for 0%

profile of v1, /device:TPU:8, one launch (start us, length us, event | category | flops | bytes accessed | tf_op | source)
XLA Modules:
  0.0 679.3 jit_solution(15825059955726146211)
XLA Ops:
  7.2 1.2 compare_select_fusion.2
  9.4 1.3 fusion.30
  12.0 1.5 constant_dynamic-slice_fusion.3
  16.0 1.5 fusion.43
  19.4 65.3 %all-gather.5.cloned.1.call-done = bf16[64,1,200,3,128]{4,2,3,1,0:T(8,128)(2,1)} async-done(((bf16[2,1,200,3,128]{4,2,3,1,0:T(8,128)(2,1)}), bf16[64,1,200,3,128]{4,2,3,1,0:T(8,128)(2,1)}) %all-gather.5.cloned.1.call-update) | async-done | bytes 9830416 | tf_op jit(solution)/shard_map/all_gather | solution.py:80
  84.7 9.3 %fusion.39 = (bf16[32,1,1,200,3,128]{5,3,4,2,1,0:T(8,128)(2,1)}, bf16[32,1,1,200,3,128]{5,3,4,2,1,0:T(8,128)(2,1)}) fusion(bf16[32,2,1,200,3,128]{5,3,4,2,1,0:T(8,128)(2,1)} %bitcast.230), kind=kLoop, calls=%fused_computation.131 | loop fusion | bytes 19660800 | tf_op jit(solution)/shard_map/slice | solution.py:81
  94.1 1.0 select_bitcast_fusion.3
  96.1 1.0 bitcast_select_fusion
  97.8 1.3 copy.28
  101.6 1.1 reshape.540
  105.3 52.3 %all-gather.7.cloned.1.call-done = bf16[64,1,200,3,14]{2,4,3,1,0:T(8,128)(2,1)} async-done(((bf16[2,1,200,3,14]{2,4,3,1,0:T(8,128)(2,1)}), bf16[64,1,200,3,14]{2,4,3,1,0:T(8,128)(2,1)}) %all-gather.7.cloned.1.call-update) | async-done | bytes 1075216 | tf_op jit(solution)/shard_map/all_gather | solution.py:91
  157.6 28.8 %copy.29 = bf16[64,1,200,3,14]{3,2,4,0,1:T(8,128)(2,1)} copy(bf16[64,1,200,3,14]{2,4,3,1,0:T(8,128)(2,1)} %all-gather.7.cloned.1.call-done) | data formatting | bytes 2150400 | tf_op jit(solution)/shard_map/all_gather | solution.py:91
  186.4 30.0 %fusion.38 = (bf16[32,1,1,200,3,14]{4,3,5,2,1,0:T(8,128)(2,1)}, bf16[32,1,1,200,3,14]{4,3,5,2,1,0:T(8,128)(2,1)}) fusion(bf16[32,2,1,200,3,14]{4,3,5,2,1,0:T(8,128)(2,1)} %bitcast.229), kind=kLoop, calls=%fused_computation.130 | loop fusion | bytes 2150400 | tf_op jit(solution)/shard_map/slice | solution.py:92
  216.3 1.4 select_bitcast_fusion
  218.1 1.8 maximum_convert_fusion
  220.3 11.7 %fusion.37 = (f32[8,128]{1,0:T(8,128)S(1)}, f32[1,200,8,128]{3,1,2,0:T(8,128)S(1)}) fusion(f32[1,200,14,134]{3,1,2,0:T(8,128)S(1)} %maximum_convert_fusion, f32[200]{0:T(256)S(1)} %bitcast.247, f32[200]{0:T(256)S(1)} %bitcast.248, f32[200]{0:T(256)S(1)} %bitcast.250, f32[200]{0:T(256)S(1)} %bitcast.251, f32[200]{0:T(256)S(1)} %bitcast.252, ...), kind=kLoop, calls=%fused_computation.129 | loop fusion | flops 20069376 | bytes 41003296 | tf_op jit(solution)/shard_map/reduce_sum | solution.py:105
  233.4 1.5 fusion.28
  236.1 1.7 fusion.5
  237.8 1.8 fusion.26
  239.6 1.6 fusion.13
  241.2 2.2 copy.34
  243.7 2.1 fusion.17
  246.0 5.3 multiply_reduce_fusion
  251.3 139.2 %all-reduce.7.cloned.1.call-done = (f32[200,800]{1,0:T(8,128)}, f32[800,200]{0,1:T(8,128)}) async-done(((f32[200,800]{1,0:T(8,128)}, f32[800,200]{0,1:T(8,128)}), (f32[200,800]{1,0:T(8,128)}, f32[800,200]{0,1:T(8,128)})) %all-reduce.7.cloned.1.call-update) | async-done | bytes 1280016 | tf_op jit(solution)/shard_map/psum | solution.py:14
  390.6 4.6 multiply_reduce_fusion.36
  395.2 4.7 multiply_reduce_fusion.18
  400.0 50.8 %psum.46 = f32[200,49]{0,1:T(8,128)S(1)} all-reduce(f32[200,49]{0,1:T(8,128)S(1)} %stack.223), channel_id=1, replica_groups=mesh['ens'=8,'tile'=32] {'ens'}, use_global_device_ids=true, to_apply=%region_58.59 | all-reduce | flops 9800 | bytes 78400 | tf_op jit(solution)/shard_map/psum | solution.py:14
  450.8 133.3 %psum.47 = f32[200,49]{0,1:T(8,128)S(1)} all-reduce(f32[200,49]{0,1:T(8,128)S(1)} %psum.46), channel_id=1, replica_groups=mesh['ens'=8,'tile'=32] {'tile'}, use_global_device_ids=true, to_apply=%region_59.60 | all-reduce | flops 9800 | bytes 78400 | tf_op jit(solution)/shard_map/psum | solution.py:14
  584.7 2.5 add_convert_fusion
  587.2 81.5 %all-reduce.5.cloned.1.call-done = (f32[200,800]{1,0:T(8,128)}, f32[800,200]{0,1:T(8,128)}) async-done(((f32[200,800]{1,0:T(8,128)}, f32[800,200]{0,1:T(8,128)}), (f32[200,800]{1,0:T(8,128)}, f32[800,200]{0,1:T(8,128)})) %all-reduce.5.cloned.1.call-update) | async-done | bytes 1280016 | tf_op jit(solution)/shard_map/psum | solution.py:14
  668.7 2.0 broadcast_multiply_fusion
  670.8 2.0 broadcast_multiply_fusion.1
  (142 shorter events, 10.2 us)
Async XLA Ops:
  7.2 225.3 %copy-start = (bf16[200,800]{1,0:T(8,128)(2,1)S(1)}, bf16[200,800]{1,0:T(8,128)(2,1)}, u32[]{:S(2)}) copy-start(bf16[200,800]{1,0:T(8,128)(2,1)} %param.17) | copy-start | bytes 960004
  7.2 77.5 %all-gather.5.cloned.1.call-start = ((), (), s32[]{:S(2)}) async-start(), calls=%async_computation | async-start | bytes 10137600 | tf_op jit(solution)/shard_map/all_gather | solution.py:80
  8.5 88.6 %copy-start.4 = (bf16[1,200,8,128]{3,1,2,0:T(8,128)(2,1)}, bf16[1,200,8,128]{3,1,2,0:T(8,128)(2,1)S(1)}, u32[]{:S(2)}) copy-start(bf16[1,200,8,128]{3,1,2,0:T(8,128)(2,1)S(1)} %compare_select_fusion.2) | copy-start | bytes 1228804
  9.3 148.2 %all-gather.7.cloned.1.call-start = ((), (), s32[]{:S(2)}) async-start(), calls=%async_computation.1 | async-start | bytes 1622016 | tf_op jit(solution)/shard_map/all_gather | solution.py:91
  97.1 3.5 copy-start.5
  97.4 4.2 copy-start.10
  97.4 5.3 copy-start.13
  97.5 5.8 copy-start.11
  99.2 291.4 %all-reduce.7.cloned.1.call-start = ((), (), s32[]{:S(2)}) async-start(), calls=%async_computation.3 | async-start | bytes 2867200 | tf_op jit(solution)/shard_map/psum | solution.py:14
  217.8 2.2 copy-start.15
  217.8 2.2 copy-start.16
  217.8 2.2 copy-start.17
  217.8 2.2 copy-start.18
  217.8 2.2 copy-start.19
  217.8 2.2 copy-start.20
  217.8 2.2 copy-start.21
  217.8 2.2 copy-start.22
  217.8 2.2 copy-start.23
  217.9 2.2 copy-start.24
  217.9 2.2 copy-start.25
  217.9 2.2 copy-start.26
  217.9 2.2 copy-start.27
  217.9 2.2 copy-start.28
  217.9 2.2 copy-start.29
  217.9 2.2 copy-start.30
  220.3 11.9 %copy-start.14 = (f32[200]{0:T(256)S(1)}, f32[200]{0:T(256)}, u32[]{:S(2)}) copy-start(f32[200]{0:T(256)} %param.16) | copy-start | bytes 2404
  233.3 2.4 copy-start.6
  233.4 2.4 copy-start.9
  233.4 2.4 copy-start.12
  233.4 2.4 copy-start.53
  243.4 425.3 %all-reduce.5.cloned.1.call-start = ((), (), s32[]{:S(2)}) async-start(), calls=%async_computation.2 | async-start | bytes 2867200 | tf_op jit(solution)/shard_map/psum | solution.py:14
  390.6 4.6 copy-start.3
  (27 other events, 55.2 us)
Sparse Core Ops, SparseCore 0:
  10.4 74.2 all-gather.4
  99.3 58.2 all-gather.6
  243.5 146.9 all-reduce.6
  393.1 275.5 all-reduce.4
